TPU v7x, 1024 devices: a whole 4x4x32 slice. The times are simulated.
1024 devices in a mesh: grp: 4 (over y), seq: 32 (over x, z_lo), rep: 8 (over z_hi, core).
Axes of the slice: x: 4, y: 4, z: 32 (z_hi: 4, z_lo: 8; z = z_hi * 8 + z_lo), core: 2. Of those that a mesh axis runs over, the one named last changes fastest.
Arguments:
- query_rows: bfloat16 [8, 4, 4096, 2560], P('rep', 'grp', 'seq'), may hold values from -8 to 8
- key_rows: bfloat16 [8, 4, 4096, 2560], P('rep', 'grp', 'seq'), may hold values from -8 to 8
- value_rows: bfloat16 [8, 4, 4096, 2560], P('rep', 'grp', 'seq'), may hold values from -6 to 6
- view_frame: int32 [8, 4, 4096], P('rep', 'grp', 'seq'), may hold values from 0 to 39, never falling along the last dimension, each value on 1 to 128 neighbouring positions
- control_row: int32 [8, 4, 4096], P('rep', 'grp', 'seq'), may hold values from 0 to 4095, as said below
- control_gate: float32 [2560], P('rep'), may hold values from 0.2 to 1.6
- out_grad: bfloat16 [8, 4, 4096, 2560], P('rep', 'grp', 'seq'), may hold values from -6 to 6
Outputs:
- block_out: bfloat16 [8, 4, 4096, 2560], P('rep', 'grp', 'seq')
- branch_grad: bfloat16 [8, 4096, 2560], P('rep', 'seq')
Inputs may be any that keep to these rules, and one draw needn't show every extreme that they name: `view_frame`: values never fall along a sequence; value // 20 is the camera and value % 20 the frame; one value holds at most 128 positions. `control_row`: position t of a sequence takes a row r with r // 128 == t // 128.
All inputs are finite; a program needn't handle non-finite values.
Results may differ from a plain program's by a relative error of at most 0.0057.
Values may be sent and summed in bfloat16 or wider, within the bound.
A program may use at most 64 MiB of HBM per device.

v0:
```python
import math

import jax
import jax.numpy as jnp
from jax import lax
from jax.sharding import Mesh
from jax.sharding import PartitionSpec as P

HEADS = 32
DH = 80
FRAMES = 20
SEQ = ("seq_0", "seq_1")


def in_order(parts, dim):
    parts = jnp.moveaxis(parts, 0, dim)
    dims = parts.shape
    return parts.reshape(*dims[:dim], dims[dim] * dims[dim + 1], *dims[dim + 2 :])


def from_everyone(x, axis):
    copies = jnp.broadcast_to(x, (lax.axis_size(axis), *x.shape))
    return lax.all_to_all(copies, axis, split_axis=0, concat_axis=0, tiled=True)


def gathered_copies(x, axis, dim):
    return in_order(from_everyone(x, axis), dim)


def gathered_by_axis(x, axes, dim):
    whole = x
    for number in range(len(axes) - 1, -1, -1):
        whole = lax.all_gather(whole, axes[number], axis=dim, tiled=True)
    return whole


def shifted(block, axis, distance):
    devices = range(lax.axis_size(axis))
    route = [(i - distance, i) for i in devices if i - distance in devices]
    return lax.ppermute(block, axis, route)


def broadcast(x, axis, root):
    return lax.dynamic_index_in_dim(lax.all_gather(x, axis), root, 0, keepdims=False)


def taken_together(x, axis):
    return from_everyone(x, axis).sum(axis=0)


def attend(queries, keys_pad, values_pad, query_tag, key_tag, frame_count, block_rows):
    length = queries.shape[-1]
    factor = 1.0 / math.sqrt(queries.shape[1])

    def one_block(block_index):
        query_seg = query_tag - 1
        key_seg = key_tag - 1
        allowed = (
            (key_seg[None, :] >= 0)
            & (query_seg[:, None] // frame_count == key_seg[None, :] // frame_count)
            & (jnp.abs(query_seg[:, None] - key_seg[None, :]) <= 1)
        )
        scores = (
            jnp.einsum("hdq,hdk->hqk", queries, keys_pad, preferred_element_type=jnp.float32)
            * factor
        )
        scores = jnp.where(allowed[None], scores, -1e30)
        largest = jnp.max(scores, axis=-1, keepdims=True)
        powers = jnp.exp(scores - largest)
        totals = jnp.sum(powers, axis=-1, keepdims=True)
        weights = (powers / totals).astype(jnp.bfloat16)
        mixed_rows = jnp.einsum(
            "hqk,hdk->hdq", weights, values_pad, preferred_element_type=jnp.float32
        )
        return mixed_rows.astype(jnp.bfloat16)

    blocks = lax.map(one_block, jnp.arange(length // block_rows, dtype=jnp.int32))
    heads_count = queries.shape[0]
    return jnp.moveaxis(blocks, 0, 2).reshape(heads_count, queries.shape[1], length)


def local(query_rows, key_rows, value_rows, view_frame, control_row, control_gate, out_grad):
    queries = query_rows[0, 0]
    token_count = queries.shape[0]
    width = queries.shape[1]
    length = token_count * lax.axis_size(SEQ)
    reach = 2 * (length // 32)
    full_gate = gathered_copies(control_gate, "rep", 0)
    tags = gathered_by_axis(view_frame[0, 0] + 1, SEQ, 0)
    shaped = (token_count, HEADS, DH)

    def head_major(rows_in):
        return rows_in.reshape(shaped).transpose(1, 2, 0)

    paired = jnp.stack((head_major(key_rows[0, 0]), head_major(value_rows[0, 0])), axis=0)
    hops = (reach + token_count - 1) // token_count
    lower_list = []
    upper_list = []
    moving_low = paired
    moving_high = paired
    for hop in range(hops):
        moving_low = shifted(moving_low, SEQ, 1)
        moving_high = shifted(moving_high, SEQ, -1)
        lower_list.insert(0, moving_low)
        upper_list.append(moving_high)
    window_rows = jnp.concatenate(lower_list + [paired] + upper_list, axis=3)
    position = lax.axis_index(SEQ)
    tag_pad = jnp.pad(tags, (hops * token_count, hops * token_count))
    key_tag = lax.dynamic_slice_in_dim(
        tag_pad, position * token_count, (2 * hops + 1) * token_count, 0
    )
    query_tag = lax.dynamic_slice_in_dim(tags, position * token_count, token_count, 0)
    group_size = 8
    group_count = HEADS // group_size
    window_len = window_rows.shape[3]
    grouped_query = head_major(queries).reshape(group_count, group_size, DH, token_count)
    grouped_key = window_rows[0].reshape(group_count, group_size, DH, window_len)
    grouped_value = window_rows[1].reshape(group_count, group_size, DH, window_len)

    def one_group(packed):
        group_query, group_key, group_value = packed
        return attend(group_query, group_key, group_value, query_tag, key_tag, FRAMES, token_count)

    attended = lax.map(one_group, (grouped_query, grouped_key, grouped_value))
    own_rows = (
        attended.reshape(HEADS, DH, token_count).transpose(2, 0, 1).reshape(token_count, width)
    )
    branch_rows = broadcast(own_rows, "grp", 0)
    local_rows = control_row[0, 0] % token_count
    selector = (local_rows[:, None] == jnp.arange(token_count, dtype=jnp.int32)[None, :]).astype(
        jnp.bfloat16
    )
    relayed = jnp.dot(selector, branch_rows, preferred_element_type=jnp.float32)
    block_out = (own_rows.astype(jnp.float32) + full_gate * relayed).astype(jnp.bfloat16)
    grads = out_grad[0, 0]
    summed = jnp.dot(selector.T, grads, preferred_element_type=jnp.float32)
    own_term = jnp.where(lax.axis_index("grp") == 0, grads.astype(jnp.float32), 0.0)
    branch_sum = taken_together(full_gate * summed + own_term, "grp")
    return (block_out[None, None], branch_sum.astype(jnp.bfloat16)[None])


def solution(mesh):
    torus = Mesh(
        mesh.devices.reshape(mesh.shape["grp"], 4, 8, mesh.shape["rep"]),
        ("grp", "seq_0", "seq_1", "rep"),
    )
    return jax.shard_map(
        local,
        mesh=torus,
        in_specs=(
            P("rep", "grp", SEQ, None),
            P("rep", "grp", SEQ, None),
            P("rep", "grp", SEQ, None),
            P("rep", "grp", SEQ),
            P("rep", "grp", SEQ),
            P("rep"),
            P("rep", "grp", SEQ, None),
        ),
        out_specs=(P("rep", "grp", SEQ, None), P("rep", SEQ, None)),
        check_vma=False,
    )
```

profile of v0, /device:TPU:1, one launch (start us, length us, event | category | flops | bytes accessed | tf_op | source)
XLA Modules:
  0.0 252.0 jit_solution(18312540104689250365)
XLA Ops:
  7.2 0.0 copy-start.1
  7.2 0.0 copy-start.2
  7.2 1.4 copy.22
  8.6 0.0 copy-start.3
  8.6 0.0 copy-start
  8.6 1.5 copy.23
  10.1 1.2 pad_maximum_fusion
  11.3 5.4 %collective-permute-start = (bf16[2,32,80,128]{3,2,1,0:T(8,128)(2,1)}, bf16[2,32,80,128]{3,2,1,0:T(8,128)(2,1)}, u32[]{:S(2)}, u32[]{:S(2)}) collective-permute-start(bf16[2,32,80,128]{3,2,1,0:T(8,128)(2,1)} %pad_maximum_fusion), channel_id=1, source_target_pairs={{0,8},{8,16},{16,24},{24,32},{32,40},{40,48},{48,56},{56,64},{64,7... | collective-permute-start | bytes 3932168 | tf_op jit(solution)/shard_map/ppermute | solution.py:40
  16.7 1.3 collective-permute-start.2
  18.0 15.3 %collective-permute-done = bf16[2,32,80,128]{3,2,1,0:T(8,128)(2,1)} collective-permute-done((bf16[2,32,80,128]{3,2,1,0:T(8,128)(2,1)}, bf16[2,32,80,128]{3,2,1,0:T(8,128)(2,1)}, u32[]{:S(2)}, u32[]{:S(2)}) %collective-permute-start) | collective-permute-done | bytes 1310752 | tf_op jit(solution)/shard_map/ppermute | solution.py:40
  33.3 14.7 %collective-permute-start.1 = (bf16[2,32,80,128]{3,2,1,0:T(8,128)(2,1)}, bf16[2,32,80,128]{3,2,1,0:T(8,128)(2,1)}, u32[]{:S(2)}, u32[]{:S(2)}) collective-permute-start(bf16[2,32,80,128]{3,2,1,0:T(8,128)(2,1)} %collective-permute-done), channel_id=1, source_target_pairs={{0,8},{8,16},{16,24},{24,32},{32,40},{40,48},{48,56},{56,64},{64,7... | collective-permute-start | bytes 3932168 | tf_op jit(solution)/shard_map/ppermute | solution.py:40
  48.1 0.0 copy-done.1
  48.1 0.6 broadcast_in_dim.69
  48.7 29.8 %all-to-all-start = ((f32[8,1,320]{2,1,0:T(1,128)}), f32[8,1,320]{2,1,0:T(1,128)S(1)}, u32[]{:S(2)}, u32[]{:S(2)}) async-start(f32[8,1,320]{2,1,0:T(1,128)} %broadcast_in_dim.69), calls=%async_computation | async-start | bytes 24576 | tf_op jit(solution)/shard_map/all_to_all | solution.py:23
  78.5 0.0 copy-done.2
  78.5 42.9 %all-gather = s32[1,1,1024]{2,1,0:T(1,128)S(1)} all-gather(s32[1,1,128]{2,1,0:T(1,128)S(1)} %broadcast_add_fusion.2), channel_id=2, replica_groups=mesh['grp'=4,'seq_0'=4,'seq_1'=8,'rep'=8] {'seq_1'}, dimensions={2}, use_global_device_ids=true | all-gather | bytes 4608 | tf_op jit(solution)/shard_map/all_gather | solution.py:33
  121.4 0.0 collective-permute-done.2
  121.4 1.3 collective-permute-start.3
  122.7 2.2 copy.24
  124.9 14.8 %all-gather.1 = s32[1,1,4096]{2,1,0:T(1,128)S(1)} all-gather(s32[1,1,1024]{2,1,0:T(1,128)S(1)} %all-gather), channel_id=3, replica_groups=mesh['grp'=4,'seq_0'=4,'seq_1'=8,'rep'=8] {'seq_0'}, dimensions={2}, use_global_device_ids=true | all-gather | bytes 20480 | tf_op jit(solution)/shard_map/all_gather | solution.py:33
  139.6 0.1 pad_dynamic-slice_fusion
  139.7 0.0 copy-done.3
  139.7 0.0 all-to-all-done
  139.8 0.1 mul.33
  139.8 0.0 copy-done
  139.8 0.4 fusion.51
  140.3 3.0 %broadcast_in_dim.72 = f32[4,128,2560]{2,1,0:T(8,128)} broadcast(f32[128,2560]{1,0:T(8,128)S(1)} %fusion.51), dimensions={1,2} | broadcast | bytes 6553600 | tf_op jit(solution)/shard_map/broadcast_in_dim | solution.py:22
  143.3 5.0 %all-to-all-start.1 = ((f32[4,128,2560]{2,1,0:T(8,128)}), f32[4,128,2560]{2,1,0:T(8,128)}, u32[]{:S(2)}, u32[]{:S(2)}) async-start(f32[4,128,2560]{2,1,0:T(8,128)} %broadcast_in_dim.72), calls=%async_computation.1 | async-start | bytes 10485760 | tf_op jit(solution)/shard_map/all_to_all | solution.py:23
  148.3 0.0 all-gather.4.cloned.1.call-start
  148.4 0.0 collective-permute-done.1
  148.4 1.5 constant_dynamic-update-slice_fusion.4
  149.9 1.6 constant_dynamic-update-slice_fusion.3
  151.6 0.3 constant_dynamic-update-slice_fusion.2
  151.9 0.3 constant_dynamic-update-slice_fusion.1
  152.2 0.0 collective-permute-done.3
  152.2 1.6 constant_dynamic-update-slice_fusion
  153.8 2.4 fusion.64
  156.2 22.7 %while.17 = (s32[]{:T(128)}, bf16[4,8,80,128]{3,2,1,0:T(8,128)(2,1)}, bf16[4,8,80,640]{3,2,1,0:T(8,128)(2,1)}, s32[640]{0:T(1024)S(1)}, s32[128]{0:T(128)S(1)}, ...) while((s32[]{:T(128)}, bf16[4,8,80,128]{3,2,1,0:T(8,128)(2,1)}, ...), condition=%wide.region_3.4_spmd, body=%wide.region_0.3_spmd.sunk | while | flops 321054976 | bytes 3225429 | solution.py:124
  156.3 0.2 fusion.78
  156.5 2.1 fusion.79
  158.5 3.4 %fusion.80 = bf16[4,8,80,128]{3,2,1,0:T(8,128)(2,1)} fusion(bf16[4,8,80,128]{3,2,1,0:T(8,128)(2,1)} %get-tuple-element.218, s32[]{:T(128)} %get-tuple-element.217, f32[8,128]{1,0:T(8,128)S(1)} %fusion.79, bf16[4,8,80,640]{3,2,1,0:T(8,128)(2,1)} %get-tuple-element.227, pred[128,640]{1,0:T(8,128)(4,1)S(1)} %fusion.78, ...), kind=kOutput, calls=%fused_computation.11.clone.1 | convolution fusion | flops 213075584 | bytes 2054144 | tf_op jit(solution)/shard_map/while/body/eval_jaxpr/while/body/eval_jaxpr/hqk,hdk->hdq/dot_general | solution.py:72
  161.9 0.2 fusion.78
  162.1 2.1 fusion.79
  164.2 3.4 %fusion.80 = bf16[4,8,80,128]{3,2,1,0:T(8,128)(2,1)} fusion(bf16[4,8,80,128]{3,2,1,0:T(8,128)(2,1)} %get-tuple-element.218, s32[]{:T(128)} %get-tuple-element.217, f32[8,128]{1,0:T(8,128)S(1)} %fusion.79, bf16[4,8,80,640]{3,2,1,0:T(8,128)(2,1)} %get-tuple-element.227, pred[128,640]{1,0:T(8,128)(4,1)S(1)} %fusion.78, ...), kind=kOutput, calls=%fused_computation.11.clone.1 | convolution fusion | flops 213075584 | bytes 2054144 | tf_op jit(solution)/shard_map/while/body/eval_jaxpr/while/body/eval_jaxpr/hqk,hdk->hdq/dot_general | solution.py:72
  167.6 0.2 fusion.78
  167.8 2.1 fusion.79
  169.9 3.4 %fusion.80 = bf16[4,8,80,128]{3,2,1,0:T(8,128)(2,1)} fusion(bf16[4,8,80,128]{3,2,1,0:T(8,128)(2,1)} %get-tuple-element.218, s32[]{:T(128)} %get-tuple-element.217, f32[8,128]{1,0:T(8,128)S(1)} %fusion.79, bf16[4,8,80,640]{3,2,1,0:T(8,128)(2,1)} %get-tuple-element.227, pred[128,640]{1,0:T(8,128)(4,1)S(1)} %fusion.78, ...), kind=kOutput, calls=%fused_computation.11.clone.1 | convolution fusion | flops 213075584 | bytes 2054144 | tf_op jit(solution)/shard_map/while/body/eval_jaxpr/while/body/eval_jaxpr/hqk,hdk->hdq/dot_general | solution.py:72
  173.3 0.2 fusion.78
  173.5 2.1 fusion.79
  175.6 3.4 %fusion.80 = bf16[4,8,80,128]{3,2,1,0:T(8,128)(2,1)} fusion(bf16[4,8,80,128]{3,2,1,0:T(8,128)(2,1)} %get-tuple-element.218, s32[]{:T(128)} %get-tuple-element.217, f32[8,128]{1,0:T(8,128)S(1)} %fusion.79, bf16[4,8,80,640]{3,2,1,0:T(8,128)(2,1)} %get-tuple-element.227, pred[128,640]{1,0:T(8,128)(4,1)S(1)} %fusion.78, ...), kind=kOutput, calls=%fused_computation.11.clone.1 | convolution fusion | flops 213075584 | bytes 2054144 | tf_op jit(solution)/shard_map/while/body/eval_jaxpr/while/body/eval_jaxpr/hqk,hdk->hdq/dot_general | solution.py:72
  178.9 2.2 copy.25
  181.1 0.0 all-gather.4.cloned.1.call-update
  181.1 1.2 bitcast_convert_fusion
  182.3 0.4 copy.26
  182.7 17.9 %all-to-all-done.1 = f32[4,128,2560]{2,1,0:T(8,128)} async-done(((f32[4,128,2560]{2,1,0:T(8,128)}), f32[4,128,2560]{2,1,0:T(8,128)}, u32[]{:S(2)}, u32[]{:S(2)}) %all-to-all-start.1) | async-done | bytes 5242912 | tf_op jit(solution)/shard_map/all_to_all | solution.py:23
  200.6 3.9 %reduce_sum.23 = bf16[128,2560]{1,0:T(8,128)(2,1)} reduce(f32[4,128,2560]{2,1,0:T(8,128)} %all-to-all-done.1, f32[]{:T(128)} %constant.133.clone.1), dimensions={0}, to_apply=%region_4.5 | reduce | flops 983040 | bytes 5898244 | tf_op jit(solution)/shard_map/reduce_sum | solution.py:48
  204.5 38.3 %all-gather.4.cloned.1.call-done = bf16[4,128,2560]{2,1,0:T(8,128)(2,1)} async-done(((bf16[1,128,2560]{2,1,0:T(8,128)(2,1)}), bf16[4,128,2560]{2,1,0:T(8,128)(2,1)}) %all-gather.4.cloned.1.call-update) | async-done | bytes 2621456 | tf_op jit(solution)/shard_map/all_gather | solution.py:44
  242.9 2.3 fusion.54
  (17 shorter events, 0.2 us)
Async XLA Ops:
  7.2 40.9 %copy-start.1 = (f32[320]{0:T(512)S(1)}, f32[320]{0:T(512)}, u32[]{:S(2)}) copy-start(f32[320]{0:T(512)} %param.14) | copy-start | bytes 3844
  7.2 71.3 %copy-start.2 = (s32[1,1,128]{2,1,0:T(1,128)S(1)}, s32[1,1,128]{2,1,0:T(1,128)}, u32[]{:S(2)}) copy-start(s32[1,1,128]{2,1,0:T(1,128)} %param.12) | copy-start | bytes 1540
  8.6 131.1 %copy-start.3 = (s32[1,1,128]{2,1,0:T(1,128)S(1)}, s32[1,1,128]{2,1,0:T(1,128)}, u32[]{:S(2)}) copy-start(s32[1,1,128]{2,1,0:T(1,128)} %param.13) | copy-start | bytes 1540
  8.6 131.2 %copy-start = (bf16[1,1,128,2560]{3,2,1,0:T(8,128)(2,1)S(1)}, bf16[1,1,128,2560]{3,2,1,0:T(8,128)(2,1)}, u32[]{:S(2)}) copy-start(bf16[1,1,128,2560]{3,2,1,0:T(8,128)(2,1)} %param.15) | copy-start | bytes 1966084
  11.3 22.0 %collective-permute-start = (bf16[2,32,80,128]{3,2,1,0:T(8,128)(2,1)}, bf16[2,32,80,128]{3,2,1,0:T(8,128)(2,1)}, u32[]{:S(2)}, u32[]{:S(2)}) collective-permute-start(bf16[2,32,80,128]{3,2,1,0:T(8,128)(2,1)} %pad_maximum_fusion), channel_id=1, source_target_pairs={{0,8},{8,16},{16,24},{24,32},{32,40},{40,48},{48,56},{56,64},{64,7... | collective-permute-start | bytes 3932168 | tf_op jit(solution)/shard_map/ppermute | solution.py:40
  16.7 104.7 %collective-permute-start.2 = (bf16[2,32,80,128]{3,2,1,0:T(8,128)(2,1)}, bf16[2,32,80,128]{3,2,1,0:T(8,128)(2,1)S(1)}, u32[]{:S(2)}, u32[]{:S(2)}) collective-permute-start(bf16[2,32,80,128]{3,2,1,0:T(8,128)(2,1)} %pad_maximum_fusion), channel_id=1, source_target_pairs={{8,0},{16,8},{24,16},{32,24},{40,32},{48,40},{56,48},{64,56},{72,6... | collective-permute-start | bytes 3932168 | tf_op jit(solution)/shard_map/ppermute | solution.py:40
  33.3 115.0 %collective-permute-start.1 = (bf16[2,32,80,128]{3,2,1,0:T(8,128)(2,1)}, bf16[2,32,80,128]{3,2,1,0:T(8,128)(2,1)}, u32[]{:S(2)}, u32[]{:S(2)}) collective-permute-start(bf16[2,32,80,128]{3,2,1,0:T(8,128)(2,1)} %collective-permute-done), channel_id=1, source_target_pairs={{0,8},{8,16},{16,24},{24,32},{32,40},{40,48},{48,56},{56,64},{64,7... | collective-permute-start | bytes 3932168 | tf_op jit(solution)/shard_map/ppermute | solution.py:40
  48.7 91.0 %all-to-all-start = ((f32[8,1,320]{2,1,0:T(1,128)}), f32[8,1,320]{2,1,0:T(1,128)S(1)}, u32[]{:S(2)}, u32[]{:S(2)}) async-start(f32[8,1,320]{2,1,0:T(1,128)} %broadcast_in_dim.69), calls=%async_computation | async-start | bytes 24576 | tf_op jit(solution)/shard_map/all_to_all | solution.py:23
  121.4 30.8 %collective-permute-start.3 = (bf16[2,32,80,128]{3,2,1,0:T(8,128)(2,1)S(1)}, bf16[2,32,80,128]{3,2,1,0:T(8,128)(2,1)}, u32[]{:S(2)}, u32[]{:S(2)}) collective-permute-start(bf16[2,32,80,128]{3,2,1,0:T(8,128)(2,1)S(1)} %collective-permute-done.2), channel_id=1, source_target_pairs={{8,0},{16,8},{24,16},{32,24},{40,32},{48,40},{56,48},{64,56},{72,6... | collective-permute-start | bytes 3932168 | tf_op jit(solution)/shard_map/ppermute | solution.py:40
  143.3 57.4 %all-to-all-start.1 = ((f32[4,128,2560]{2,1,0:T(8,128)}), f32[4,128,2560]{2,1,0:T(8,128)}, u32[]{:S(2)}, u32[]{:S(2)}) async-start(f32[4,128,2560]{2,1,0:T(8,128)} %broadcast_in_dim.72), calls=%async_computation.1 | async-start | bytes 10485760 | tf_op jit(solution)/shard_map/all_to_all | solution.py:23
  148.3 94.5 %all-gather.4.cloned.1.call-start = ((), (), s32[]{:S(2)}) async-start(), calls=%async_computation.2 | async-start | bytes 3276800 | tf_op jit(solution)/shard_map/all_gather | solution.py:44
Sparse Core Ops, SparseCore 0:
  181.2 61.5 all-gather.3
where the time goes:
time: 253 us; the launch traced here: 252 us
  waiting for transfers between devices  71.6 us (28%)
  starting transfers between devices  57.6 us (23%)
  blocking collectives  57.6 us (23%)
  matrix products  24.4 us (10%)
  local copies, waits for them, and re-layouts  18.9 us (7%)
  between operations  14.2 us (6%)
  other arithmetic  7.58 us (3%)
    all_gather x2, blocking collectives, gathered_by_axis(): whole = lax.all_gather(whole, axes[number], axis=dim, tiled=True)  57.6 us
    all_gather x1, waiting for transfers between devices, broadcast(): lax.all_gather(x, axis)  38.3 us
    all_to_all x2, starting transfers between devices, from_everyone(): return lax.all_to_all(copies, axis, split_axis=0, concat_axis=0, tiled=True)  34.9 us
    ppermute x4, starting transfers between devices, shifted(): return lax.ppermute(block, axis, route)  22.7 us
    all_to_all x2, waiting for transfers between devices, from_everyone(): return lax.all_to_all(copies, axis, split_axis=0, concat_axis=0, tiled=True)  17.9 us
    ppermute x4, waiting for transfers between devices, shifted(): return lax.ppermute(block, axis, route)  15.3 us
    dot_general x4, matrix products, one_block(): jnp.einsum('hqk,hdk->hdq', weights, values_pad, preferred_element_type=jn...  13.4 us
    unnamed x14, local copies, waits for them, and re-layouts  8.56 us
  transfers between devices with their start and end apart: 7, of which 3 were waited for; matrix products, arithmetic and copies ran while one was open for 18% of the time, Pallas kernels for 0%

commit v1 on v0

v1 whole, which is shorter than its diff:
```python
import functools
import math

import jax
import jax.numpy as jnp
from jax import lax
from jax.experimental import pallas as pl
from jax.experimental.pallas import tpu as pltpu
from jax.sharding import PartitionSpec as P

DH = 80
LANES = 128
CHUNK = 640
HEADS_CHUNK = CHUNK // DH
PARTS = (
    (range(0, 5), (0, 384)),
    (range(5, 8), (384, 256)),
)
RUN = 8
QUARTER = 32
ROWS = 128
WINDOW = 5 * ROWS
ABSENT = -1000
MESH = pl.DeviceIdType.MESH
SCALE = math.log2(math.e) / math.sqrt(DH)
OWN, LOWER, UPPER = 2, (1, 0), (3, 4)


def head_spans(head):
    first, last = head * DH, head * DH + DH
    spans = []
    for block in range(first // LANES, (last + LANES - 1) // LANES):
        low = max(first - block * LANES, 0)
        high = min(last - block * LANES, LANES)
        spans.append((block, low, high))
    return spans


def kernel(
    chunks,
    q_hbm,
    k_hbm,
    v_hbm,
    tag_ref,
    ctrl_ref,
    gate_ref,
    grad_hbm,
    out_ref,
    bgrad_ref,
    q_buf,
    k_win,
    v_win,
    tags,
    ctrls,
    gates,
    grads,
    bias,
    select,
    bounce,
    carry_buf,
    attended,
    branch,
    kv_send,
    kv_recv,
    cross_send,
    bounce_recv,
    pass_send,
    tag_send,
    tag_recv,
    gate_send,
    gate_recv,
    grad_send,
    grad_recv,
    ctrl_send,
    ctrl_recv,
    br_send,
    br_recv,
    local_sem,
):
    p = lax.axis_index("seq")
    grp = lax.axis_index("grp")
    rep = lax.axis_index("rep")
    length = lax.axis_size("seq")
    groups = lax.axis_size("grp")
    core, far = rep % 2, rep // 2
    n_far = lax.axis_size("rep") // 2
    far_up, far_down, far_two = (far + 1) % n_far, (far + n_far - 1) % n_far, (far + 2) % n_far
    sibling = far * 2 + 1 - core
    has_low, has_high = p >= 1, p <= length - 2
    inner = has_low & has_high
    low2, high2 = p >= 2, p <= length - 3
    place, column, n_columns = p % RUN, p // RUN, length // RUN
    first, last, second, late = place == 0, place == RUN - 1, place == 1, place == RUN - 2
    edge, side = first | last, first | last | second | late
    left, right = column >= 1, column <= n_columns - 2
    side_left, side_right = side & left, side & right
    crosses = (
        (last & right, late & right),
        (first & left, second & left),
    )
    through = (column + 1, n_columns - column)
    passes = ((last & left, late & left), (first & right, second & right))
    passed = (column, n_columns - 1 - column)
    relays = (inner & ~last, inner & ~first)

    barrier = pltpu.get_barrier_semaphore()

    def greet(**where):
        pl.semaphore_signal(barrier, inc=1, device_id=where, device_id_type=MESH)

    @pl.when(has_low)
    def _():
        greet(seq=p - 1)

    @pl.when(has_high)
    def _():
        greet(seq=p + 1)

    @pl.when(low2)
    def _():
        greet(seq=p - 2)

    @pl.when(high2)
    def _():
        greet(seq=p + 2)

    for there, distance in (
        (first, RUN - 1),
        (last, 1 - RUN),
        (first | second, RUN - 2),
        (last | late, 2 - RUN),
        (side_left, -RUN),
        (side_right, RUN),
    ):

        @pl.when(there)
        def _(distance=distance):
            greet(seq=p + distance)

    for step in range(1, groups):
        greet(grp=(grp + step) % groups)
    greet(rep=sibling)
    greet(rep=far_up * 2 + core)
    greet(rep=far_down * 2 + core)
    near = groups - 1 + 3

    own_rows = pl.ds(OWN * ROWS, ROWS)
    locals_ = [
        pltpu.make_async_copy(q_hbm, q_buf, local_sem.at[0]),
        pltpu.make_async_copy(k_hbm, k_win.at[own_rows, :], local_sem.at[1]),
        pltpu.make_async_copy(v_hbm, v_win.at[own_rows, :], local_sem.at[2]),
        pltpu.make_async_copy(grad_hbm, grads.at[grp], local_sem.at[3]),
        pltpu.make_async_copy(ctrl_ref, ctrls.at[grp], local_sem.at[4]),
        pltpu.make_async_copy(gate_ref, gates.at[core, far], local_sem.at[5]),
        pltpu.make_async_copy(tag_ref, tags.at[OWN], local_sem.at[6]),
    ]
    for copy in locals_:
        copy.start()

    def fill(block):
        rows = pl.ds(block * ROWS, ROWS)
        k_win[rows, :] = jnp.zeros((ROWS, k_win.shape[1]), k_win.dtype)
        v_win[rows, :] = jnp.zeros((ROWS, v_win.shape[1]), v_win.dtype)
        tags[block] = jnp.full((1, ROWS), ABSENT, jnp.int32)

    for absent, block in (
        (~has_low, LOWER[0]),
        (~low2, LOWER[1]),
        (~has_high, UPPER[0]),
        (~high2, UPPER[1]),
    ):

        @pl.when(absent)
        def _(block=block):
            fill(block)

    peers = near
    for there in (has_low, has_high, low2, high2, edge, side, side_left, side_right):
        peers = peers + there.astype(jnp.int32)
    pl.semaphore_wait(barrier, peers)

    def columns(chunk, span=(0, CHUNK)):
        start = chunk * CHUNK + span[0]
        if not isinstance(start, int):
            start = pl.multiple_of(start, LANES)
        return pl.ds(start, span[1])

    def kv_copy(way, hop, chunk, part):
        cols = columns(chunk)
        land = (LOWER, UPPER)[way]
        win, hbm = ((k_win, k_hbm), (v_win, v_hbm))[part]
        source = hbm.at[:, cols] if hop == 0 else win.at[pl.ds(land[0] * ROWS, ROWS), cols]
        return pltpu.make_async_remote_copy(
            src_ref=source,
            dst_ref=win.at[pl.ds(land[hop] * ROWS, ROWS), cols],
            send_sem=kv_send.at[way, hop, chunk, part],
            recv_sem=kv_recv.at[way, hop, chunk, part, 0],
            device_id={"seq": p + (1, -1)[way]},
            device_id_type=MESH,
        )

    def cross_copy(way, hop, chunk, part, piece, detour):
        cols = columns(chunk)
        rows = pl.ds(piece * QUARTER, QUARTER)
        if detour:
            target = bounce.at[part, rows, cols]
            arrived, where = bounce_recv.at[chunk, part, piece], p + (RUN, -RUN)[way]
        else:
            block = (LOWER, UPPER)[way][hop]
            target = (k_win, v_win)[part].at[pl.ds(block * ROWS + piece * QUARTER, QUARTER), cols]
            arrived = kv_recv.at[way, hop, chunk, part, piece]
            where = p + (hop + 1, -hop - 1)[way]
        return pltpu.make_async_remote_copy(
            src_ref=(k_hbm, v_hbm)[part].at[rows, cols],
            dst_ref=target,
            send_sem=cross_send.at[chunk, part, piece],
            recv_sem=arrived,
            device_id={"seq": where},
            device_id_type=MESH,
        )

    def pass_copy(way, hop, chunk, part, piece):
        cols = columns(chunk)
        block = (LOWER, UPPER)[way][hop]
        rows = pl.ds(block * ROWS + piece * QUARTER, QUARTER)
        return pltpu.make_async_remote_copy(
            src_ref=bounce.at[part, pl.ds(piece * QUARTER, QUARTER), cols],
            dst_ref=(k_win, v_win)[part].at[rows, cols],
            send_sem=pass_send.at[chunk, part, piece],
            recv_sem=kv_recv.at[way, hop, chunk, part, piece],
            device_id={"seq": p + (1 + hop - RUN, RUN - 1 - hop)[way]},
            device_id_type=MESH,
        )

    def tag_copy(way, hop):
        return pltpu.make_async_remote_copy(
            src_ref=tag_ref,
            dst_ref=tags.at[(LOWER, UPPER)[way][hop]],
            send_sem=tag_send.at[way, hop],
            recv_sem=tag_recv.at[way, hop],
            device_id={"seq": p + (hop + 1, -hop - 1)[way]},
            device_id_type=MESH,
        )

    tag_sends = ((0, 0, has_high), (0, 1, high2), (1, 0, has_low), (1, 1, low2))
    tag_arrivals = ((0, 0, has_low), (0, 1, low2), (1, 0, has_high), (1, 1, high2))

    def on_crossing(chunk, act):
        for way in range(2):
            for hop in range(2):
                for piece in range(4):
                    direct = piece >= through[way]

                    @pl.when(crosses[way][hop] & direct)
                    def _(way=way, hop=hop, piece=piece):
                        for part in range(2):
                            act(cross_copy(way, hop, chunk, part, piece, False))

                    if piece < 3:

                        @pl.when(crosses[way][hop] & ~direct)
                        def _(way=way, hop=hop, piece=piece):
                            for part in range(2):
                                act(cross_copy(way, hop, chunk, part, piece, True))

    def on_own(chunk, act):
        for way, there in ((0, has_high & ~last), (1, has_low & ~first)):

            @pl.when(there)
            def _(way=way):
                for part in range(2):
                    act(kv_copy(way, 0, chunk, part))

    def on_relay(chunk, act):
        for way in range(2):

            @pl.when(relays[way])
            def _(way=way):
                for part in range(2):
                    act(kv_copy(way, 1, chunk, part))

    def on_arrival(way, hop, chunk):
        in_edge = (first, last)[way]

        @pl.when(~in_edge)
        def _():
            for part in range(2):
                kv_copy(way, hop, chunk, part).wait_recv()

        @pl.when(in_edge)
        def _():
            for piece in range(4):
                for part in range(2):
                    cross_copy(way, hop, chunk, part, piece, False).wait_recv()

    def start(copy):
        copy.start()

    def left_(copy):
        copy.wait_send()

    def own_send(chunk):
        on_crossing(chunk, start)
        on_own(chunk, start)

    def relay(chunk):
        for way, here in ((0, has_low), (1, has_high)):

            @pl.when(here)
            def _(way=way):
                on_arrival(way, 0, chunk)

        on_relay(chunk, start)

    def arrive(chunk):
        for way, here in ((0, low2), (1, high2)):

            @pl.when(here)
            def _(way=way):
                on_arrival(way, 1, chunk)

    def on_pass(chunk, act):
        for way in range(2):
            for hop in range(2):
                for piece in range(3):

                    @pl.when(passes[way][hop] & (piece < passed[way]))
                    def _(way=way, hop=hop, piece=piece):
                        for part in range(2):
                            act(way, hop, chunk, part, piece)

    def forward(way, hop, chunk, part, piece):
        cross_copy(way, hop, chunk, part, piece, True).wait_recv()
        pass_copy(way, hop, chunk, part, piece).start()

    def forwarded(way, hop, chunk, part, piece):
        pass_copy(way, hop, chunk, part, piece).wait_send()

    def gate_copy(piece, target, slot, source=None):
        return pltpu.make_async_remote_copy(
            src_ref=gates.at[core, piece] if source is None else source,
            dst_ref=gates.at[core, piece],
            send_sem=gate_send.at[slot],
            recv_sem=gate_recv.at[core, piece],
            device_id={"rep": target},
            device_id_type=MESH,
        )

    to_up, to_down = far_up * 2 + core, far_down * 2 + core
    gate_copies = [
        gate_copy(far, to_up, 0, gate_ref),
        gate_copy(far, to_down, 1, gate_ref),
        gate_copy(far, sibling, 2, gate_ref),
        gate_copy(far_down, to_up, 3),
        gate_copy(far_down, sibling, 4),
        gate_copy(far_up, sibling, 5),
        gate_copy(far_two, sibling, 6),
    ]

    def gate_arrival(which, piece):
        return pltpu.make_async_remote_copy(
            src_ref=gate_ref,
            dst_ref=gates.at[which, piece],
            send_sem=gate_send.at[0],
            recv_sem=gate_recv.at[which, piece],
            device_id={"rep": sibling},
            device_id_type=MESH,
        )

    def grad_copy(step):
        return pltpu.make_async_remote_copy(
            src_ref=grad_hbm,
            dst_ref=grads.at[grp],
            send_sem=grad_send.at[step - 1],
            recv_sem=grad_recv.at[grp],
            device_id={"grp": (grp + step) % groups},
            device_id_type=MESH,
        )

    def ctrl_copy(step):
        return pltpu.make_async_remote_copy(
            src_ref=ctrl_ref,
            dst_ref=ctrls.at[grp],
            send_sem=ctrl_send.at[step - 1],
            recv_sem=ctrl_recv.at[grp],
            device_id={"grp": (grp + step) % groups},
            device_id_type=MESH,
        )

    def grad_arrival(step):
        source = (grp + step) % groups
        for src, dst, sem in ((grad_hbm, grads, grad_recv), (ctrl_ref, ctrls, ctrl_recv)):
            pltpu.make_async_remote_copy(
                src_ref=src,
                dst_ref=dst.at[source],
                send_sem=grad_send.at[0],
                recv_sem=sem.at[source],
                device_id={"grp": source},
                device_id_type=MESH,
            ).wait_recv()

    def branch_copy(chunk, half, step):
        cols = columns(chunk, PARTS[half][1])
        return pltpu.make_async_remote_copy(
            src_ref=branch.at[:, cols],
            dst_ref=branch.at[:, cols],
            send_sem=br_send.at[chunk, half, step - 1],
            recv_sem=br_recv.at[chunk, half],
            device_id={"grp": step},
            device_id_type=MESH,
        )

    for way, hop, there in tag_sends:

        @pl.when(there)
        def _(way=way, hop=hop):
            tag_copy(way, hop).start()

    for copy in gate_copies[:3]:
        copy.start()
    own_send(0)
    own_send(1)
    for step in range(1, groups):
        ctrl_copy(step).start()
        grad_copy(step).start()
    for copy in locals_:
        copy.wait()
    gate_arrival(core, far_down).wait_recv()
    gate_copies[3].start()
    gate_copies[4].start()
    gate_arrival(core, far_up).wait_recv()
    gate_copies[5].start()
    for chunk in range(2, chunks):
        own_send(chunk)

    for way, hop, here in tag_arrivals:

        @pl.when(here)
        def _(way=way, hop=hop):
            tag_copy(way, hop).wait_recv()

    def column_of(row):
        return jnp.broadcast_to(row.astype(jnp.float32), (ROWS, ROWS)).T

    query_tag = column_of(tags[OWN])
    for block in range(5):
        key_tag = jnp.broadcast_to(tags[block].astype(jnp.float32), (ROWS, ROWS))
        gap = jnp.abs(query_tag - key_tag)
        camera = (query_tag >= 20.0) == (key_tag >= 20.0)
        bias[:, block * ROWS : (block + 1) * ROWS] = jnp.where((gap <= 1.0) & camera, 0.0, -1e30)

    def selector(which):
        rows = lax.broadcasted_iota(jnp.int32, (ROWS, ROWS), 0)
        return jnp.where(rows == jnp.broadcast_to(ctrls[which] % ROWS, (ROWS, ROWS)), 1.0, 0.0)

    select[...] = selector(grp).T.astype(jnp.bfloat16)

    lane = lax.broadcasted_iota(jnp.int32, (ROWS, LANES), 1)

    def compute(chunk, half):
        def cols(block, count=1):
            return pl.ds(pl.multiple_of(chunk * CHUNK + block * LANES, LANES), count * LANES)

        heads, (result_first, result_width) = PARTS[half]
        pending = {}
        if half == 1:
            pending[result_first // LANES] = carry_buf[...]
        for head in heads:
            spans = head_spans(head)
            width = len(spans)
            queries = []
            for block, low, high in spans:
                part = q_buf[:, cols(block)]
                if (low, high) != (0, LANES):
                    part = jnp.where((lane >= low) & (lane < high), part, jnp.zeros_like(part))
                queries.append(part)
            query = queries[0] if width == 1 else jnp.concatenate(queries, axis=1)
            where = cols(spans[0][0], width)
            scores = lax.dot_general(
                query, k_win[:, where], (((1,), (1,)), ((), ())), preferred_element_type=jnp.float32
            )
            scores = scores + bias[...]
            largest = jnp.max(scores, axis=1, keepdims=True)
            powers = jnp.exp2((scores - largest) * SCALE)
            totals = jnp.sum(powers, axis=1, keepdims=True)
            weights = (powers * (1.0 / totals)).astype(jnp.bfloat16)
            mixed = jnp.dot(weights, v_win[:, where], preferred_element_type=jnp.float32)
            for number, (block, low, high) in enumerate(spans):
                piece = mixed[:, number * LANES : (number + 1) * LANES]
                if block in pending:
                    piece = jnp.where(lane >= low, piece, pending[block])
                if high == LANES:
                    pending.pop(block, None)
                    attended[:, cols(block)] = piece.astype(jnp.bfloat16)
                else:
                    pending[block] = piece
        if half == 0:
            ((_, carried),) = pending.items()
            carry_buf[...] = carried

        @pl.when(grp == 0)
        def _():
            done = columns(chunk, (result_first, result_width))
            branch[:, done] = attended[:, done]
            for step in range(1, groups):
                branch_copy(chunk, half, step).start()

    def gate_of(chunk):
        return jnp.concatenate([gates[0, chunk], gates[1, chunk]], axis=1)

    def finish(chunk):
        cols = columns(chunk)

        @pl.when(grp != 0)
        def _():
            for half in range(2):
                branch_copy(chunk, half, 1).wait_recv()

        relayed = jnp.dot(select[...], branch[:, cols], preferred_element_type=jnp.float32)
        mixed = attended[:, cols].astype(jnp.float32)
        out_ref[:, cols] = (mixed + gate_of(chunk) * relayed).astype(jnp.bfloat16)

    def gradient():
        for step in range(1, groups):
            grad_arrival(step)
        selectors = [selector(which).astype(jnp.bfloat16) for which in range(groups)]

        def one(chunk, carry):
            cols = columns(chunk)
            summed = jnp.zeros((ROWS, CHUNK), jnp.float32)
            for which in range(groups):
                summed = summed + jnp.dot(
                    selectors[which], grads[which, :, cols], preferred_element_type=jnp.float32
                )
            own = grads[0, :, cols].astype(jnp.float32)
            bgrad_ref[:, cols] = (own + gate_of(chunk) * summed).astype(jnp.bfloat16)
            return carry

        lax.fori_loop(0, chunks, one, 0)

    def spread(t, carry):
        on_pass(t, forward)
        relay(t)
        return carry

    lax.fori_loop(0, chunks, spread, 0)
    gate_arrival(core, far_two).wait_recv()
    gate_copies[6].start()

    def body(t, carry):
        @pl.when(t == 2)
        def _():
            for piece in range(n_far):
                gate_arrival(1 - core, piece).wait_recv()
            gradient()

        @pl.when(t < chunks)
        def _():
            arrive(t)
            for half in range(2):
                compute(t, half)

        @pl.when(t >= 2)
        def _():
            finish(t - 2)

        return carry

    lax.fori_loop(0, chunks + 2, body, 0)

    for way, hop, there in tag_sends:

        @pl.when(there)
        def _(way=way, hop=hop):
            tag_copy(way, hop).wait_send()

    def drain(chunk, carry):
        on_crossing(chunk, left_)
        on_own(chunk, left_)
        on_relay(chunk, left_)
        on_pass(chunk, forwarded)
        return carry

    lax.fori_loop(0, chunks, drain, 0)

    for copy in gate_copies:
        copy.wait_send()
    for step in range(1, groups):
        ctrl_copy(step).wait_send()
        grad_copy(step).wait_send()

    @pl.when(grp == 0)
    def _():
        for chunk in range(chunks):
            for half in range(2):
                for step in range(1, groups):
                    branch_copy(chunk, half, step).wait_send()


def local(query_rows, key_rows, value_rows, view_frame, control_row, control_gate, out_grad):
    q, k, v, g = query_rows[0, 0], key_rows[0, 0], value_rows[0, 0], out_grad[0, 0]
    rows, width = q.shape
    chunks = width // CHUNK
    groups = lax.axis_size("grp")
    n_far = lax.axis_size("rep") // 2
    piece = control_gate.shape[0]
    bf16, f32, i32 = jnp.bfloat16, jnp.float32, jnp.int32
    whole = pl.BlockSpec(memory_space=pltpu.VMEM)
    away = pl.BlockSpec(memory_space=pltpu.HBM)
    dma = pltpu.SemaphoreType.DMA
    out, bgrad = pl.pallas_call(
        functools.partial(kernel, chunks),
        out_shape=(
            jax.ShapeDtypeStruct((rows, width), bf16),
            jax.ShapeDtypeStruct((rows, width), bf16),
        ),
        in_specs=[away, away, away, whole, whole, whole, away],
        out_specs=(whole, whole),
        scratch_shapes=[
            pltpu.VMEM((rows, width), bf16),
            pltpu.VMEM((WINDOW, width), bf16),
            pltpu.VMEM((WINDOW, width), bf16),
            pltpu.VMEM((5, 1, rows), i32),
            pltpu.VMEM((groups, 1, rows), i32),
            pltpu.VMEM((2, n_far, 1, piece), f32),
            pltpu.VMEM((groups, rows, width), bf16),
            pltpu.VMEM((rows, WINDOW), f32),
            pltpu.VMEM((rows, rows), bf16),
            pltpu.VMEM((2, 3 * QUARTER, width), bf16),
            pltpu.VMEM((rows, LANES), f32),
            pltpu.VMEM((rows, width), bf16),
            pltpu.VMEM((rows, width), bf16),
            dma((2, 2, chunks, 2)),
            dma((2, 2, chunks, 2, 4)),
            dma((chunks, 2, 4)),
            dma((chunks, 2, 3)),
            dma((chunks, 2, 3)),
            dma((2, 2)),
            dma((2, 2)),
            dma((7,)),
            dma((2, n_far)),
            dma((groups - 1,)),
            dma((groups,)),
            dma((groups - 1,)),
            dma((groups,)),
            dma((chunks, 2, groups - 1)),
            dma((chunks, 2)),
            dma((7,)),
        ],
        compiler_params=pltpu.CompilerParams(
            collective_id=0, has_side_effects=True, vmem_limit_bytes=67_000_000
        ),
    )(
        q,
        k,
        v,
        view_frame.reshape(1, rows),
        control_row.reshape(1, rows),
        control_gate.reshape(1, piece),
        g,
    )
    return out[None, None], bgrad[None]


def solution(mesh):
    seq3 = P("rep", "grp", "seq")
    seq4 = P("rep", "grp", "seq", None)
    return jax.shard_map(
        local,
        mesh=mesh,
        in_specs=(seq4, seq4, seq4, seq3, seq3, P("rep"), seq4),
        out_specs=(seq4, P("rep", "seq", None)),
        check_vma=False,
    )
```

time: 253 us -> 147 us (0.58)
  the two profiles are of different devices: /device:TPU:1 before, /device:TPU:18 now
where the time goes in v1:
time: 147 us; the launch traced here: 146 us
  Pallas kernels  142 us (97%)
  local copies, waits for them, and re-layouts  4.11 us (3%)
    pallas_call x1, Pallas kernels, local(): pl.pallas_call(functools.partial(kernel, chunks), out_shape=(jax.ShapeDty...  142 us
    unnamed x6, local copies, waits for them, and re-layouts  3.55 us

profile of v1, /device:TPU:18, one launch (start us, length us, event | category | flops | bytes accessed | tf_op | source)
XLA Modules:
  0.0 146.4 jit_solution(1677369442149390108)
XLA Ops:
  0.6 0.0 copy-start.1
  0.6 0.7 copy-done.1
  1.3 0.6 reshape.15.gate_ref
  1.9 141.6 %shard_map.86 = (bf16[128,2560]{1,0:T(8,128)(2,1)}, bf16[128,2560]{1,0:T(8,128)(2,1)}) custom-call(bf16[128,2560]{1,0:T(8,128)(2,1)} %bitcast.10, bf16[128,2560]{1,0:T(8,128)(2,1)} %bitcast.11, bf16[128,2560]{1,0:T(8,128)(2,1)} %bitcast.12, s32[1,128]{1,0:T(1,128)} %bitcast.14, s32[1,128]{1,0:T(1,128)} %bitcast.15, f32[1,320]{1,0:T(1,128)} %reshape.15.gate_ref, ...), custom_call_target="tpu_custom_call" | custom-call | tf_op jit(solution)/shard_map/pallas_call | solution.py:611
  143.5 0.0 copy-start
  143.5 2.0 %copy.11 = bf16[1,1,128,2560]{3,2,1,0:T(8,128)(2,1)} copy(bf16[1,1,128,2560]{3,2,1,0:T(8,128)(2,1)} %bitcast.9) | data formatting | bytes 1310720
  145.5 0.0 copy-done
  145.5 0.8 copy.12
Async XLA Ops:
  0.6 0.7 copy-start.1
  143.5 2.0 %copy-start = (bf16[128,2560]{1,0:T(8,128)(2,1)S(1)}, bf16[128,2560]{1,0:T(8,128)(2,1)}, u32[]{:S(2)}) copy-start(bf16[128,2560]{1,0:T(8,128)(2,1)} %get-tuple-element.5) | copy-start | bytes 1966084

commit v2 on v1

--- a/solution.py
+++ b/solution.py
@@ -69,6 +69,8 @@
     tag_recv,
     gate_send,
     gate_recv,
+    spoke_send,
+    spoke_recv,
     grad_send,
     grad_recv,
     ctrl_send,
@@ -102,6 +104,8 @@
     passes = ((last & left, late & left), (first & right, second & right))
     passed = (column, n_columns - 1 - column)
     relays = (inner & ~last, inner & ~first)
+    hub = place == RUN // 2
+    spokes = [offset - RUN // 2 for offset in range(RUN) if offset != RUN // 2]
 
     barrier = pltpu.get_barrier_semaphore()
 
@@ -139,10 +143,20 @@
 
     for step in range(1, groups):
         greet(grp=(grp + step) % groups)
-    greet(rep=sibling)
-    greet(rep=far_up * 2 + core)
-    greet(rep=far_down * 2 + core)
-    near = groups - 1 + 3
+
+    @pl.when(hub)
+    def _():
+        greet(rep=sibling)
+        greet(rep=far_up * 2 + core)
+        greet(rep=far_down * 2 + core)
+        for offset in spokes:
+            greet(seq=p + offset)
+
+    @pl.when(~hub)
+    def _():
+        greet(seq=column * RUN + RUN // 2)
+
+    near = groups - 1 + jnp.where(hub, 3 + len(spokes), 1)
 
     own_rows = pl.ds(OWN * ROWS, ROWS)
     locals_ = [
@@ -151,11 +165,15 @@
         pltpu.make_async_copy(v_hbm, v_win.at[own_rows, :], local_sem.at[2]),
         pltpu.make_async_copy(grad_hbm, grads.at[grp], local_sem.at[3]),
         pltpu.make_async_copy(ctrl_ref, ctrls.at[grp], local_sem.at[4]),
-        pltpu.make_async_copy(gate_ref, gates.at[core, far], local_sem.at[5]),
         pltpu.make_async_copy(tag_ref, tags.at[OWN], local_sem.at[6]),
     ]
+    gate_local = pltpu.make_async_copy(gate_ref, gates.at[core, far], local_sem.at[5])
     for copy in locals_:
         copy.start()
+
+    @pl.when(hub)
+    def _():
+        gate_local.start()
 
     def fill(block):
         rows = pl.ds(block * ROWS, ROWS)
@@ -367,6 +385,16 @@
             device_id_type=MESH,
         )
 
+    def spread_copy(number):
+        return pltpu.make_async_remote_copy(
+            src_ref=gates,
+            dst_ref=gates,
+            send_sem=spoke_send.at[number],
+            recv_sem=spoke_recv,
+            device_id={"seq": p + spokes[number]},
+            device_id_type=MESH,
+        )
+
     def grad_copy(step):
         return pltpu.make_async_remote_copy(
             src_ref=grad_hbm,
@@ -416,8 +444,11 @@
         def _(way=way, hop=hop):
             tag_copy(way, hop).start()
 
-    for copy in gate_copies[:3]:
-        copy.start()
+    @pl.when(hub)
+    def _():
+        for copy in gate_copies[:3]:
+            copy.start()
+
     own_send(0)
     own_send(1)
     for step in range(1, groups):
@@ -425,12 +456,28 @@
         grad_copy(step).start()
     for copy in locals_:
         copy.wait()
-    gate_arrival(core, far_down).wait_recv()
-    gate_copies[3].start()
-    gate_copies[4].start()
-    gate_arrival(core, far_up).wait_recv()
-    gate_copies[5].start()
-    for chunk in range(2, chunks):
+
+    @pl.when(hub)
+    def _():
+        gate_local.wait()
+        gate_arrival(core, far_down).wait_recv()
+        gate_copies[3].start()
+        gate_copies[4].start()
+        gate_arrival(core, far_up).wait_recv()
+        gate_copies[5].start()
+
+    own_send(2)
+
+    @pl.when(hub)
+    def _():
+        gate_arrival(core, far_two).wait_recv()
+        gate_copies[6].start()
+        for piece in range(n_far):
+            gate_arrival(1 - core, piece).wait_recv()
+        for number in range(len(spokes)):
+            spread_copy(number).start()
+
+    for chunk in range(3, chunks):
         own_send(chunk)
 
     for way, hop, here in tag_arrivals:
@@ -544,14 +591,14 @@
         return carry
 
     lax.fori_loop(0, chunks, spread, 0)
-    gate_arrival(core, far_two).wait_recv()
-    gate_copies[6].start()
 
     def body(t, carry):
         @pl.when(t == 2)
         def _():
-            for piece in range(n_far):
-                gate_arrival(1 - core, piece).wait_recv()
+            @pl.when(~hub)
+            def _():
+                spread_copy(0).wait_recv()
+
             gradient()
 
         @pl.when(t < chunks)
@@ -583,8 +630,13 @@
 
     lax.fori_loop(0, chunks, drain, 0)
 
-    for copy in gate_copies:
-        copy.wait_send()
+    @pl.when(hub)
+    def _():
+        for copy in gate_copies:
+            copy.wait_send()
+        for number in range(len(spokes)):
+            spread_copy(number).wait_send()
+
     for step in range(1, groups):
         ctrl_copy(step).wait_send()
         grad_copy(step).wait_send()
@@ -639,6 +691,8 @@
             dma((2, 2)),
             dma((7,)),
             dma((2, n_far)),
+            dma((RUN - 1,)),
+            dma,
             dma((groups - 1,)),
             dma((groups,)),
             dma((groups - 1,)),

time: 147 us -> 147 us (level)
  the two profiles are of different devices: /device:TPU:18 before, /device:TPU:119 now
where the time goes in v2:
time: 147 us
  Pallas kernels  142 us (97%)
  local copies, waits for them, and re-layouts  4.11 us (3%)
    pallas_call x1, Pallas kernels, local(): pl.pallas_call(functools.partial(kernel, chunks), out_shape=(jax.ShapeDty...  142 us
    unnamed x6, local copies, waits for them, and re-layouts  3.55 us

profile of v2, /device:TPU:119, one launch (start us, length us, event | category | flops | bytes accessed | tf_op | source)
XLA Modules:
  0.0 146.8 jit_solution(343589711447297401)
XLA Ops:
  0.6 0.0 copy-start.1
  0.6 0.7 copy-done.1
  1.3 0.6 reshape.15.gate_ref
  1.9 142.0 %shard_map.86 = (bf16[128,2560]{1,0:T(8,128)(2,1)}, bf16[128,2560]{1,0:T(8,128)(2,1)}) custom-call(bf16[128,2560]{1,0:T(8,128)(2,1)} %bitcast.10, bf16[128,2560]{1,0:T(8,128)(2,1)} %bitcast.11, bf16[128,2560]{1,0:T(8,128)(2,1)} %bitcast.12, s32[1,128]{1,0:T(1,128)} %bitcast.14, s32[1,128]{1,0:T(1,128)} %bitcast.15, f32[1,320]{1,0:T(1,128)} %reshape.15.gate_ref, ...), custom_call_target="tpu_custom_call" | custom-call | tf_op jit(solution)/shard_map/pallas_call | solution.py:663
  143.9 0.0 copy-start
  143.9 2.0 %copy.11 = bf16[1,1,128,2560]{3,2,1,0:T(8,128)(2,1)} copy(bf16[1,1,128,2560]{3,2,1,0:T(8,128)(2,1)} %bitcast.9) | data formatting | bytes 1310720
  146.0 0.0 copy-done
  146.0 0.8 copy.12
Async XLA Ops:
  0.6 0.7 copy-start.1
  143.9 2.0 %copy-start = (bf16[128,2560]{1,0:T(8,128)(2,1)S(1)}, bf16[128,2560]{1,0:T(8,128)(2,1)}, u32[]{:S(2)}) copy-start(bf16[128,2560]{1,0:T(8,128)(2,1)} %get-tuple-element.5) | copy-start | bytes 1966084
